TPU v7x, 32 devices: a whole 2x2x4 slice. The times are simulated.
32 devices in a mesh: dp: 4 (over y, x), section: 2 (over core), tensor: 4 (over z).
Axes of the slice: x: 2, y: 2, z: 4, core: 2. Of those that a mesh axis runs over, the one named last changes fastest.
Arguments:
- stored: bfloat16 [2, 2, 256, 8192], P('section', None, 'dp', 'tensor'), may hold values from -6 to 6
- cotangent: bfloat16 [2, 32, 8192], P(None, None, 'tensor'), may hold values from -12 to 12
- positions: int32 [2, 32], replicated, may hold values from 128 to 255, as said below
- lengths: int32 [2], replicated, may hold values from 128 to 256, as said below
- norm_gain: float32 [2, 8192], P('section'), may hold values from 0.5 to 1.5
- w_query: bfloat16 [2, 8192, 8192], P('section', None, 'tensor')
- w_key: bfloat16 [2, 8192, 1024], P('section', None, 'tensor')
- w_value: bfloat16 [2, 8192, 1024], P('section', None, 'tensor'), may hold values from -0.0625 to 0.0625
- w_out: bfloat16 [2, 8192, 8192], P('section', 'tensor', 'dp'), may hold values from -0.0625 to 0.0625
Outputs:
- input_grads: float32 [2, 2, 256, 8192], P('section', None, 'dp', 'tensor')
Inputs may be any that keep to these rules, and one draw needn't show every extreme that they name: In each sequence the response positions are distinct, rise along the last dimension, lie in the last 128 positions, and the last one is 255. `lengths`: some sequence has length 256.
All inputs are finite; a program needn't handle non-finite values.
Results may differ from a plain program's by a relative error of at most 0.017.
Values may be sent and summed in bfloat16 or wider, within the bound.
A program may use at most 256 MiB of HBM per device.

v0:
```python
import math
import jax
import jax.numpy as jnp
from jax import lax
from jax.sharding import PartitionSpec as P

HD = 128
EPS = 1e-05
THETA = 500000.0


def passed_along(value, axis, steps):
    count = lax.axis_size(axis)
    leading, last = (max(0, -steps), min(count, count - steps))
    return lax.ppermute(value, axis, [(source, source + steps) for source in range(leading, last)])


def angle_tables(row_places):
    half_dim = HD // 2
    frequency = THETA ** (-(jnp.arange(half_dim, dtype=jnp.float32) * 2.0) / HD)
    angles = row_places[:, None] * frequency[None, :]
    cosine = jnp.concatenate([jnp.cos(angles), jnp.cos(angles)], -1)[:, None, :]
    sine_table = jnp.concatenate([jnp.sin(angles), jnp.sin(angles)], -1)[:, None, :]
    return (cosine, sine_table)


def turn_half(values):
    half_dim = values.shape[-1] // 2
    return jnp.concatenate([-values[..., half_dim:], values[..., :half_dim]], -1)


def rotate(values, cosine, sine_table):
    return values * cosine + turn_half(values) * sine_table


def unrotate(values, cosine, sine_table):
    return values * cosine - turn_half(values * sine_table)


def layer_grad(own_input, own_upstream, seq_lengths, gain, w_query, w_key, w_value, w_out):
    batch, rows, width_dev = own_input.shape
    kv_dev = w_key.shape[1] // HD
    q_dev = w_query.shape[1] // HD
    group = q_dev // kv_dev
    scale = 1.0 / math.sqrt(HD)
    x_whole, g_whole = (
        lax.all_gather(own_input, "tensor", axis=2, tiled=True),
        lax.all_gather(own_upstream, "tensor", axis=2, tiled=True),
    )
    width = x_whole.shape[2]
    x_full = x_whole.astype(jnp.float32)
    inv_rms = lax.rsqrt(jnp.mean(x_full * x_full, -1, keepdims=True) + EPS)
    normed = (x_full * inv_rms * gain).astype(jnp.bfloat16)
    first_row = lax.axis_index("dp") * rows
    query_ids = first_row + jnp.arange(rows, dtype=jnp.int32)
    cosine, sine_table = angle_tables(query_ids.astype(jnp.float32))
    queries = jnp.einsum(
        "bpd,dc->bpc", normed, w_query, preferred_element_type=jnp.float32
    ).reshape(batch, rows, q_dev, HD)
    keys = jnp.einsum("bpd,dc->bpc", normed, w_key, preferred_element_type=jnp.float32).reshape(
        batch, rows, kv_dev, HD
    )
    values = jnp.einsum("bpd,dc->bpc", normed, w_value, preferred_element_type=jnp.float32).reshape(
        batch, rows, kv_dev, HD
    )
    q_rot = rotate(queries, cosine, sine_table).astype(jnp.bfloat16)
    k_rot = rotate(keys, cosine, sine_table).astype(jnp.bfloat16)
    values_b = values.astype(jnp.bfloat16)
    grad_out = jnp.einsum("bpd,cd->bpc", g_whole, w_out, preferred_element_type=jnp.float32).astype(
        jnp.bfloat16
    )
    all_keys, all_values = (
        lax.all_gather(k_rot, "dp", axis=1, tiled=True),
        lax.all_gather(values_b, "dp", axis=1, tiled=True),
    )
    length = all_keys.shape[1]
    q_five = q_rot.reshape(batch, rows, kv_dev, group, HD)
    o_five = grad_out.reshape(batch, rows, kv_dev, group, HD)
    key_ids = jnp.arange(length, dtype=jnp.int32)
    causal = key_ids[None, None, :] <= query_ids[None, :, None]
    start_pos = length - seq_lengths
    inside = (key_ids[None, None, :] >= start_pos[:, None, None]) | (
        key_ids[None, None, :] == query_ids[None, :, None]
    )
    allowed = (causal & inside)[:, None, None, :, :]
    scores = (
        jnp.einsum("bpkgd,bjkd->bkgpj", q_five, all_keys, preferred_element_type=jnp.float32)
        * scale
    )
    masked = jnp.where(allowed, scores, -1e30)
    highest = jnp.max(masked, -1, keepdims=True)
    expo_terms = jnp.where(allowed, jnp.exp(masked - highest), 0.0)
    probs = expo_terms / jnp.sum(expo_terms, -1, keepdims=True)
    grad_probs = jnp.einsum(
        "bpkgd,bjkd->bkgpj", o_five, all_values, preferred_element_type=jnp.float32
    )
    row_dot = jnp.sum(probs * grad_probs, -1, keepdims=True)
    grad_scores = (probs * (grad_probs - row_dot) * scale).astype(jnp.bfloat16)
    probs_b = probs.astype(jnp.bfloat16)
    grad_qr = jnp.einsum(
        "bkgpj,bjkd->bpkgd", grad_scores, all_keys, preferred_element_type=jnp.float32
    )
    key_terms = jnp.einsum(
        "bkgpj,bpkgd->bjkd", grad_scores, q_five, preferred_element_type=jnp.float32
    )
    value_terms = jnp.einsum(
        "bkgpj,bpkgd->bjkd", probs_b, o_five, preferred_element_type=jnp.float32
    )
    grad_kr, grad_vr = (
        lax.psum_scatter(
            key_terms.astype(jnp.bfloat16), "dp", scatter_dimension=1, tiled=True
        ).astype(jnp.float32),
        lax.psum_scatter(
            value_terms.astype(jnp.bfloat16), "dp", scatter_dimension=1, tiled=True
        ).astype(jnp.float32),
    )
    grad_q = (
        unrotate(grad_qr.reshape(batch, rows, q_dev, HD), cosine, sine_table)
        .astype(jnp.bfloat16)
        .reshape(batch, rows, q_dev * HD)
    )
    grad_k = (
        unrotate(grad_kr, cosine, sine_table).astype(jnp.bfloat16).reshape(batch, rows, kv_dev * HD)
    )
    grad_v = grad_vr.astype(jnp.bfloat16).reshape(batch, rows, kv_dev * HD)
    partial_term = jnp.einsum("bpc,dc->bpd", grad_q, w_query, preferred_element_type=jnp.float32)
    partial_term = partial_term + jnp.einsum(
        "bpc,dc->bpd", grad_k, w_key, preferred_element_type=jnp.float32
    )
    partial_term = partial_term + jnp.einsum(
        "bpc,dc->bpd", grad_v, w_value, preferred_element_type=jnp.float32
    )
    summed = lax.psum(partial_term.astype(jnp.bfloat16), "tensor").astype(jnp.float32)
    stat = jnp.sum(x_full * gain * summed, -1, keepdims=True)
    whole_grad = (
        g_whole.astype(jnp.float32) + inv_rms * gain * summed - x_full * inv_rms**3 * stat / width
    )
    return lax.dynamic_slice_in_dim(whole_grad, lax.axis_index("tensor") * width_dev, width_dev, 2)


def on_device(stored, cotangent, positions, lengths, norm_gain, w_query, w_key, w_value, w_out):
    own_input = stored[0]
    gain = norm_gain[0]
    wq_layer = w_query[0]
    wk_layer = w_key[0]
    wv_layer = w_value[0]
    wo_layer = lax.all_gather(w_out[0], "dp", axis=1, tiled=True)
    seqs, rows, width_dev = own_input.shape
    section_id = lax.axis_index("section")
    row_ids = lax.axis_index("dp") * rows + jnp.arange(rows, dtype=jnp.int32)
    placed = (positions[:, None, :] == row_ids[None, :, None]).astype(jnp.bfloat16)
    from_loss = jnp.einsum(
        "spr,srd->spd", placed, cotangent, preferred_element_type=jnp.float32
    ).astype(jnp.bfloat16)

    def run_layer(input_part, upstream_part, length_part):
        return layer_grad(
            input_part, upstream_part, length_part, gain, wq_layer, wk_layer, wv_layer, wo_layer
        )

    first_in = jnp.where(section_id == 1, from_loss, jnp.zeros_like(from_loss))
    first_pass = run_layer(own_input, first_in, lengths)
    handed = passed_along(first_pass.astype(jnp.bfloat16), "section", -1)
    second_pass = run_layer(own_input, handed, lengths)
    result = jnp.where(section_id == 0, second_pass, first_pass)
    return result[None]


def solution(mesh):
    return jax.shard_map(
        on_device,
        mesh=mesh,
        in_specs=(
            P("section", None, "dp", "tensor"),
            P(None, None, "tensor"),
            P(),
            P(),
            P("section", None),
            P("section", None, "tensor"),
            P("section", None, "tensor"),
            P("section", None, "tensor"),
            P("section", "tensor", "dp"),
        ),
        out_specs=P("section", None, "dp", "tensor"),
        check_vma=False,
    )
```

profile of v0, /device:TPU:0, one launch (start us, length us, event | category | flops | bytes accessed | tf_op | source)
XLA Modules:
  0.0 914.5 jit_solution(1680415631563956756)
XLA Ops:
  10.3 40.0 %copy.63 = bf16[2048,8192]{1,0:T(8,128)(2,1)} copy(bf16[2048,8192]{0,1:T(8,128)(2,1)} %bitcast.235) | data formatting | bytes 67108864 | tf_op jit(solution)/shard_map/bpd,dc->bpc/dot_general | solution.py:57
  50.3 6.4 copy.62
  56.7 6.4 copy.64
  71.5 10.4 %all_gather.23 = bf16[2,256,2,128]{3,1,2,0:T(8,128)(2,1)S(1)} all-gather(bf16[2,64,2,128]{3,1,2,0:T(8,128)(2,1)S(1)} %fusion.113), channel_id=1, replica_groups=mesh['dp'=4,'section'=2,'tensor'=4] {'dp'}, dimensions={1}, use_global_device_ids=true | all-gather | bytes 327680 | tf_op jit(solution)/shard_map/all_gather | solution.py:73
  83.4 9.6 %all_gather.24 = bf16[2,256,2,128]{3,1,2,0:T(8,128)(2,1)S(1)} all-gather(bf16[2,64,2,128]{3,1,2,0:T(8,128)(2,1)S(1)} %convolution_convert_fusion.1), channel_id=1, replica_groups=mesh['dp'=4,'section'=2,'tensor'=4] {'dp'}, dimensions={1}, use_global_device_ids=true | all-gather | bytes 327680 | tf_op jit(solution)/shard_map/all_gather | solution.py:74
  93.1 15.8 %fusion.115 = f32[2,64,16,128]{3,1,2,0:T(8,128)S(1)} fusion(bf16[16,128,8192,1]{2,1,0,3:T(8,128)(2,1)} %bitcast.236, bf16[1,2,64,8192]{3,2,1,0:T(8,128)(2,1)S(1)} %copy-done.2, f32[8192]{0:T(1024)S(1)} %bitcast.253, f32[2,64]{1,0:T(2,128)S(1)} %get-tuple-element.23), kind=kOutput, calls=%fused_computation.131 | convolution fusion | flops 4299161600 | bytes 36733440 | tf_op jit(solution)/shard_map/bpd,dc->bpc/dot_general | solution.py:57
  115.8 285.4 %all-gather.13.cloned.1.call-done = bf16[1,2048,8192]{2,1,0:T(8,128)(2,1)} async-done(((bf16[1,2048,2048]{2,1,0:T(8,128)(2,1)}), bf16[1,2048,8192]{2,1,0:T(8,128)(2,1)}) %all-gather.13.cloned.1.call-update) | async-done | bytes 33554448 | tf_op jit(solution)/shard_map/all_gather | solution.py:147
  401.2 16.4 %fusion.44 = bf16[2,64,2048]{2,1,0:T(8,128)(2,1)S(1)} fusion(bf16[2,64,8192]{2,1,0:T(8,128)(2,1)} %all-gather.7.cloned.1.call-done, bf16[1,2048,8192]{2,1,0:T(8,128)(2,1)} %all-gather.13.cloned.1.call-done), kind=kOutput, calls=%fused_computation.36 | convolution fusion | flops 4295229440 | bytes 36175872 | tf_op jit(solution)/shard_map/bpd,cd->bpc/dot_general | solution.py:69
  420.2 15.5 %fusion.77 = f32[2,2,128,8,64]{2,4,3,1,0:T(8,128)} fusion(f32[2,2,256,64,8]{2,3,4,1,0:T(8,128)} %fusion.96, bf16[2,256,2,128]{3,1,2,0:T(8,128)(2,1)S(1)} %all_gather.23, f32[2,2,8,64,256]{4,3,2,1,0:T(8,128)} %get-tuple-element.29, f32[2,2,8,64]{3,2,1,0:T(8,128)S(1)} %get-tuple-element.28), kind=kOutput, calls=%fused_computation.86 | convolution fusion | flops 137890048 | bytes 5513216 | tf_op jit(solution)/shard_map/bkgpj,bjkd->bpkgd/dot_general | solution.py:100
  443.0 16.3 %fusion.66 = bf16[2,256,2,128]{3,1,2,0:T(8,128)(2,1)} fusion(bf16[2,64,2,8,128]{4,1,3,2,0:T(8,128)(2,1)} %bitcast.257, f32[2,2,256,64,8]{2,3,4,1,0:T(8,128)} %fusion.96, f32[2,2,8,64,256]{4,3,2,1,0:T(8,128)} %get-tuple-element.29, f32[2,2,8,64]{3,2,1,0:T(8,128)S(1)} %get-tuple-element.28), kind=kOutput, calls=%fused_computation.66 | convolution fusion | flops 138021120 | bytes 4988928 | tf_op jit(solution)/shard_map/bkgpj,bpkgd->bjkd/dot_general | solution.py:103
  459.4 24.7 %all-reduce.11.cloned.1.call-done = bf16[2,256,2,128]{3,2,0,1:T(2,128)(2,1)} async-done(((bf16[2,256,2,128]{3,2,0,1:T(2,128)(2,1)}), bf16[2,256,2,128]{3,2,0,1:T(2,128)(2,1)}) %all-reduce.11.cloned.1.call-update) | async-done | bytes 262160
  490.8 20.3 %reduce-scatter.3.cloned.1.call-done = bf16[2,64,2,128]{3,1,2,0:T(8,128)(2,1)} async-done(((bf16[2,256,2,128]{3,1,2,0:T(8,128)(2,1)}), bf16[2,64,2,128]{3,1,2,0:T(8,128)(2,1)}) %reduce-scatter.3.cloned.1.call-update) | async-done | bytes 65552 | tf_op jit(solution)/shard_map/reduce_scatter | solution.py:110
  512.0 5.8 fusion.42
  517.8 19.2 %fusion.26 = bf16[2,64,8192]{2,1,0:T(8,128)(2,1)} fusion(f32[2,64,8192]{2,1,0:T(8,128)} %fusion.38, f32[2,64,8192]{2,1,0:T(8,128)} %fusion.42, bf16[1,8192,2048]{2,1,0:T(8,128)(2,1)} %param.14, f32[2,64,16,64]{3,1,2,0:T(8,128)} %get-tuple-element.12, f32[2,64,16,64]{3,1,2,0:T(8,128)} %get-tuple-element.11, f32[2,64,16,128]{3,1,2,0:T(8,128)S(1)} %bitcast.242, ...), kind=kOutput, calls=%fused_computation.16 | convolution fusion | flops 4299161600 | bytes 46170112 | tf_op jit(solution)/shard_map/bpc,dc->bpd/dot_general | solution.py:126
  537.1 86.2 %all-reduce.7.cloned.1.call-done = bf16[2,64,8192]{2,1,0:T(8,128)(2,1)} async-done(((bf16[2,64,8192]{2,1,0:T(8,128)(2,1)}), bf16[2,64,8192]{2,1,0:T(8,128)(2,1)}) %all-reduce.7.cloned.1.call-update) | async-done | bytes 2097168 | tf_op jit(solution)/shard_map/psum | solution.py:133
  636.0 44.6 %all-gather.9.cloned.1.call-done = bf16[2,64,8192]{2,1,0:T(8,128)(2,1)} async-done(((bf16[2,64,2048]{2,1,0:T(8,128)(2,1)}), bf16[2,64,8192]{2,1,0:T(8,128)(2,1)}) %all-gather.9.cloned.1.call-update) | async-done | bytes 2097168 | tf_op jit(solution)/shard_map/all_gather | solution.py:48
  680.6 16.4 %fusion.47 = bf16[2,64,2048]{2,1,0:T(8,128)(2,1)S(1)} fusion(bf16[2,64,8192]{2,1,0:T(8,128)(2,1)} %all-gather.9.cloned.1.call-done, bf16[1,2048,8192]{2,1,0:T(8,128)(2,1)} %all-gather.13.cloned.1.call-done), kind=kOutput, calls=%fused_computation.37 | convolution fusion | flops 4295229440 | bytes 36175872 | tf_op jit(solution)/shard_map/bpd,cd->bpc/dot_general | solution.py:69
  700.4 15.6 %fusion.79 = f32[2,2,128,8,64]{2,4,3,1,0:T(8,128)} fusion(f32[2,2,256,64,8]{2,3,4,1,0:T(8,128)} %fusion.93, bf16[2,256,2,128]{3,1,2,0:T(8,128)(2,1)S(1)} %copy-done.21, f32[2,2,8,64,256]{4,3,2,1,0:T(8,128)} %get-tuple-element.29, f32[2,2,8,64]{3,2,1,0:T(8,128)S(1)} %get-tuple-element.28), kind=kOutput, calls=%fused_computation.88 | convolution fusion | flops 137890048 | bytes 5513216 | tf_op jit(solution)/shard_map/bkgpj,bjkd->bpkgd/dot_general | solution.py:100
  721.0 16.3 %fusion.64 = bf16[2,256,2,128]{3,1,2,0:T(8,128)(2,1)} fusion(bf16[2,64,2,8,128]{4,1,3,2,0:T(8,128)(2,1)} %bitcast.258, f32[2,2,256,64,8]{2,3,4,1,0:T(8,128)} %fusion.93, f32[2,2,8,64,256]{4,3,2,1,0:T(8,128)} %get-tuple-element.29, f32[2,2,8,64]{3,2,1,0:T(8,128)S(1)} %get-tuple-element.28), kind=kOutput, calls=%fused_computation.64 | convolution fusion | flops 138021120 | bytes 4988928 | tf_op jit(solution)/shard_map/bkgpj,bpkgd->bjkd/dot_general | solution.py:103
  737.6 23.7 %all-reduce.13.cloned.1.call-done = bf16[2,256,2,128]{3,2,0,1:T(2,128)(2,1)} async-done(((bf16[2,256,2,128]{3,2,0,1:T(2,128)(2,1)}), bf16[2,256,2,128]{3,2,0,1:T(2,128)(2,1)}) %all-reduce.13.cloned.1.call-update) | async-done | bytes 262160
  767.9 20.6 %reduce-scatter.5.cloned.1.call-done = bf16[2,64,2,128]{3,1,2,0:T(8,128)(2,1)} async-done(((bf16[2,256,2,128]{3,1,2,0:T(8,128)(2,1)}), bf16[2,64,2,128]{3,1,2,0:T(8,128)(2,1)}) %reduce-scatter.5.cloned.1.call-update) | async-done | bytes 65552 | tf_op jit(solution)/shard_map/reduce_scatter | solution.py:110
  789.4 5.8 fusion.40
  795.2 19.3 %fusion.23 = bf16[2,64,8192]{2,1,0:T(8,128)(2,1)} fusion(f32[2,64,8192]{2,1,0:T(8,128)} %fusion.36, f32[2,64,8192]{2,1,0:T(8,128)} %fusion.40, bf16[1,8192,2048]{2,1,0:T(8,128)(2,1)} %param.14, f32[2,64,16,64]{3,1,2,0:T(8,128)} %get-tuple-element.10, f32[2,64,16,64]{3,1,2,0:T(8,128)} %get-tuple-element.9, f32[2,64,16,128]{3,1,2,0:T(8,128)S(1)} %bitcast.240, ...), kind=kOutput, calls=%fused_computation.15 | convolution fusion | flops 4299161600 | bytes 46170112 | tf_op jit(solution)/shard_map/bpc,dc->bpd/dot_general | solution.py:126
  814.6 86.3 %all-reduce.9.cloned.1.call-done = bf16[2,64,8192]{2,1,0:T(8,128)(2,1)} async-done(((bf16[2,64,8192]{2,1,0:T(8,128)(2,1)}), bf16[2,64,8192]{2,1,0:T(8,128)(2,1)}) %all-reduce.9.cloned.1.call-update) | async-done | bytes 2097168 | tf_op jit(solution)/shard_map/psum | solution.py:133
  (121 shorter events, 72.6 us)
Async XLA Ops:
  6.5 58.4 %all-gather.11.cloned.1.call-start = ((), (), s32[]{:S(2)}) async-start(), calls=%async_computation.8 | async-start | bytes 2621440 | tf_op jit(solution)/shard_map/all_gather | solution.py:47
  7.3 108.6 %all-gather.7.cloned.1.call-start = ((), (), s32[]{:S(2)}) async-start(), calls=%async_computation.2 | async-start | bytes 2621440 | tf_op jit(solution)/shard_map/all_gather | solution.py:48
  9.5 391.7 %all-gather.13.cloned.1.call-start = ((), (), s32[]{:S(2)}) async-start(), calls=%async_computation.9 | async-start | bytes 41943040 | tf_op jit(solution)/shard_map/all_gather | solution.py:147
  10.2 473.9 %all-reduce.11.cloned.1.call-start = ((), (), s32[]{:S(2)}) async-start(), calls=%async_computation.10 | async-start | bytes 524288
  56.7 6.4 copy-start.23
  56.7 8.0 copy-start.22
  63.1 4.2 copy-start.17
  67.4 14.5 %copy-start.9 = (bf16[256,8192]{1,0:T(8,128)(2,1)S(1)}, bf16[256,8192]{1,0:T(8,128)(2,1)}, u32[]{:S(2)}) copy-start(bf16[256,8192]{1,0:T(8,128)(2,1)} %copy.64) | copy-start | bytes 12582916
  81.9 338.3 %copy-start.20 = (bf16[2,256,2,128]{3,1,2,0:T(8,128)(2,1)}, bf16[2,256,2,128]{3,1,2,0:T(8,128)(2,1)S(1)}, u32[]{:S(2)}) copy-start(bf16[2,256,2,128]{3,1,2,0:T(8,128)(2,1)S(1)} %all_gather.23) | copy-start | bytes 786436
  93.1 324.6 %copy-start.11 = (bf16[2,256,2,128]{3,1,2,0:T(8,128)(2,1)}, bf16[2,256,2,128]{3,1,2,0:T(8,128)(2,1)S(1)}, u32[]{:S(2)}) copy-start(bf16[2,256,2,128]{3,1,2,0:T(8,128)(2,1)S(1)} %all_gather.24) | copy-start | bytes 786436
  440.7 70.3 %reduce-scatter.3.cloned.1.call-start = ((), (), s32[]{:S(2)}) async-start(), calls=%async_computation.3 | async-start | bytes 327680 | tf_op jit(solution)/shard_map/reduce_scatter | solution.py:110
  459.3 164.0 %all-reduce.7.cloned.1.call-start = ((), (), s32[]{:S(2)}) async-start(), calls=%async_computation.4 | async-start | bytes 4194304 | tf_op jit(solution)/shard_map/psum | solution.py:133
  512.0 5.8 copy-start.8
  537.1 143.5 %all-gather.9.cloned.1.call-start = ((), (), s32[]{:S(2)}) async-start(), calls=%async_computation.5 | async-start | bytes 2621440 | tf_op jit(solution)/shard_map/all_gather | solution.py:48
  627.5 3.4 copy-start.3
  627.5 3.6 copy-start.4
  631.1 3.8 collective-permute-start
  635.7 61.4 %copy-start.12 = (bf16[2,256,2,128]{3,1,2,0:T(8,128)(2,1)S(1)}, bf16[2,256,2,128]{3,1,2,0:T(8,128)(2,1)}, u32[]{:S(2)}) copy-start(bf16[2,256,2,128]{3,1,2,0:T(8,128)(2,1)} %copy-done.11) | copy-start | bytes 786436
  635.8 125.5 %all-reduce.13.cloned.1.call-start = ((), (), s32[]{:S(2)}) async-start(), calls=%async_computation.11 | async-start | bytes 524288
  697.1 3.3 copy-start.21
  719.1 69.3 %reduce-scatter.5.cloned.1.call-start = ((), (), s32[]{:S(2)}) async-start(), calls=%async_computation.6 | async-start | bytes 327680 | tf_op jit(solution)/shard_map/reduce_scatter | solution.py:110
  737.3 163.5 %all-reduce.9.cloned.1.call-start = ((), (), s32[]{:S(2)}) async-start(), calls=%async_computation.7 | async-start | bytes 4194304 | tf_op jit(solution)/shard_map/psum | solution.py:133
  789.4 5.8 copy-start.7
  904.0 3.4 copy-start.1
  (11 other events, 18.0 us)
Sparse Core Ops, SparseCore 0:
  8.9 48.3 all-gather.10
  58.9 44.4 all-gather.6
  105.3 295.8 all-gather.12
  440.9 43.1 all-reduce.10
  486.7 24.3 reduce-scatter.2
  537.2 86.1 all-reduce.6
  635.9 44.6 all-gather.8
  719.3 41.9 all-reduce.12
  764.1 24.3 reduce-scatter.4
  814.7 86.1 all-reduce.8
where the time goes:
time: 921 us; the launch traced here: 914 us
  waiting for transfers between devices  596 us (65%)
  matrix products  190 us (21%)
  local copies, waits for them, and re-layouts  62 us (7%)
  other arithmetic  29.4 us (3%)
  blocking collectives  20 us (2%)
  between operations  14.8 us (2%)
    all_gather x1, waiting for transfers between devices, on_device(): wo_layer = lax.all_gather(w_out[0], 'dp', axis=1, tiled=True)  285 us
    psum x2, waiting for transfers between devices, layer_grad(): lax.psum(partial_term.astype(jnp.bfloat16), 'tensor').astype(jnp.float32)  172 us
    unnamed x12, waiting for transfers between devices  49.9 us
    all_gather x2, waiting for transfers between devices, layer_grad(): lax.all_gather(own_upstream, 'tensor', axis=2, tiled=True)  44.6 us
    reduce_scatter x2, waiting for transfers between devices, layer_grad(): lax.psum_scatter(key_terms.astype(jnp.bfloat16), 'dp', scatter_dimension=...  40.8 us
    dot_general x1, local copies, waits for them, and re-layouts, layer_grad(): jnp.einsum('bpd,dc->bpc', normed, w_query, preferred_element_type=jnp.flo...  40 us
    dot_general x2, matrix products, layer_grad(): jnp.einsum('bpc,dc->bpd', grad_q, w_query, preferred_element_type=jnp.flo...  38.6 us
    dot_general x2, matrix products, layer_grad(): jnp.einsum('bpd,cd->bpc', g_whole, w_out, preferred_element_type=jnp.floa...  32.7 us
  transfers between devices with their start and end apart: 11, of which 9 were waited for; matrix products, arithmetic and copies ran while one was open for 15% of the time, Pallas kernels for 0%

commit v1 on v0

--- a/solution.py
+++ b/solution.py
@@ -7,6 +7,18 @@
 HD = 128
 EPS = 1e-05
 THETA = 500000.0
+
+
+def doubled_up(x, axis, dim):
+    ways, here = (lax.axis_size(axis), lax.axis_index(axis))
+    grown, reach = (x, 1)
+    while reach < ways:
+        theirs = lax.ppermute(grown, axis, [(d, d ^ reach) for d in range(ways)])
+        mine_first = jnp.concatenate([grown, theirs], axis=dim)
+        theirs_first = jnp.concatenate([theirs, grown], axis=dim)
+        grown = jnp.where(here & reach == 0, mine_first, theirs_first)
+        reach = 2 * reach
+    return grown
 
 
 def passed_along(value, axis, steps):
@@ -144,7 +156,7 @@
     wq_layer = w_query[0]
     wk_layer = w_key[0]
     wv_layer = w_value[0]
-    wo_layer = lax.all_gather(w_out[0], "dp", axis=1, tiled=True)
+    wo_layer = doubled_up(w_out[0], "dp", 1)
     seqs, rows, width_dev = own_input.shape
     section_id = lax.axis_index("section")
     row_ids = lax.axis_index("dp") * rows + jnp.arange(rows, dtype=jnp.int32)

time: 921 us -> 1160 us (1.26)
  blocking collectives: 20 us -> 310 us
  waiting for transfers between devices: 596 us -> 490 us
  matrix products: 190 us -> 224 us
  other arithmetic: 29.4 us -> 47.9 us
    all_gather x1, blocking collectives: 10.4 us -> 301 us  [layer_grad(): lax.all_gather(k_rot, 'dp', axis=1, tiled=True)]
    all_gather x1 -> x0, waiting for transfers between devices: 285 us -> none  [on_device(): wo_layer = lax.all_gather(w_out[0], 'dp', axis=1, tiled=True)]
    ppermute x0 -> x2, waiting for transfers between devices: none -> 181 us  [doubled_up(): theirs = lax.ppermute(grown, axis, [(d, d ^ reach) for d in range(ways)])]
    dot_general x2, matrix products: 32.7 us -> 65 us  [layer_grad(): jnp.einsum('bpd,cd->bpc', g_whole, w_out, preferred_element_type=jnp.floa...]
    select_n x0 -> x1, other arithmetic: none -> 20.5 us  [doubled_up(): grown = jnp.where(here & reach == 0, mine_first, theirs_first)]
    unnamed x12 -> x11, waiting for transfers between devices: 49.9 us -> 48.8 us
  transfers between devices with their start and end apart: 11 -> 12, of which waited for: 9 -> 9; matrix products, arithmetic and copies ran while one was open for 15% -> 12% of each run, Pallas kernels for 0% -> 0%
where the time goes in v1:
time: 1160 us
  waiting for transfers between devices  490 us (42%)
  blocking collectives  310 us (27%)
  matrix products  224 us (19%)
  local copies, waits for them, and re-layouts  63.6 us (5%)
  other arithmetic  47.9 us (4%)
  between operations  14.5 us (1%)
    all_gather x1, blocking collectives, layer_grad(): lax.all_gather(k_rot, 'dp', axis=1, tiled=True)  301 us
    ppermute x2, waiting for transfers between devices, doubled_up(): theirs = lax.ppermute(grown, axis, [(d, d ^ reach) for d in range(ways)])  181 us
    psum x2, waiting for transfers between devices, layer_grad(): lax.psum(partial_term.astype(jnp.bfloat16), 'tensor').astype(jnp.float32)  173 us
    dot_general x2, matrix products, layer_grad(): jnp.einsum('bpd,cd->bpc', g_whole, w_out, preferred_element_type=jnp.floa...  65 us
    unnamed x11, waiting for transfers between devices  48.8 us
    all_gather x2, waiting for transfers between devices, layer_grad(): lax.all_gather(own_upstream, 'tensor', axis=2, tiled=True)  44.6 us
    reduce_scatter x2, waiting for transfers between devices, layer_grad(): lax.psum_scatter(key_terms.astype(jnp.bfloat16), 'dp', scatter_dimension=...  40.9 us
    dot_general x1, local copies, waits for them, and re-layouts, layer_grad(): jnp.einsum('bpd,dc->bpc', normed, w_query, preferred_element_type=jnp.flo...  40.7 us
  transfers between devices with their start and end apart: 12, of which 9 were waited for; matrix products, arithmetic and copies ran while one was open for 12% of the time, Pallas kernels for 0%

profile of v1, /device:TPU:0, one launch (start us, length us, event | category | flops | bytes accessed | tf_op | source)
XLA Modules:
  0.0 1158.0 jit_solution(1821221556518108670)
XLA Ops:
  9.5 180.8 %collective-permute-done = bf16[2048,2048]{1,0:T(8,128)(2,1)} collective-permute-done((bf16[2048,2048]{1,0:T(8,128)(2,1)}, bf16[2048,2048]{1,0:T(8,128)(2,1)}, u32[]{:S(2)}, u32[]{:S(2)}) %collective-permute-start) | collective-permute-done | bytes 8388640 | tf_op jit(solution)/shard_map/ppermute | solution.py:16
  190.3 20.5 %maximum_select_fusion.1 = bf16[2048,4096]{1,0:T(8,128)(2,1)} fusion(bf16[2048,2048]{1,0:T(8,128)(2,1)} %collective-permute-done, bf16[2048,2048]{1,0:T(8,128)(2,1)} %bitcast.239, pred[]{:T(512)S(6)} %eq.53), kind=kLoop, calls=%fused_computation.11 | loop fusion | flops 75497472 | bytes 33554432 | tf_op jit(solution)/shard_map/jit(_where)/select_n | solution.py:19
  214.0 40.7 %copy.63 = bf16[2048,8192]{1,0:T(8,128)(2,1)} copy(bf16[2048,8192]{0,1:T(8,128)(2,1)} %bitcast.234) | data formatting | bytes 67108864 | tf_op jit(solution)/shard_map/bpd,dc->bpc/dot_general | solution.py:69
  254.7 6.4 copy.62
  261.0 6.5 copy.64
  276.2 300.6 %all_gather.20 = bf16[2,256,2,128]{3,1,2,0:T(8,128)(2,1)S(1)} all-gather(bf16[2,64,2,128]{3,1,2,0:T(8,128)(2,1)S(1)} %fusion.114), channel_id=1, replica_groups=mesh['dp'=4,'section'=2,'tensor'=4] {'dp'}, dimensions={1}, use_global_device_ids=true | all-gather | bytes 327680 | tf_op jit(solution)/shard_map/all_gather | solution.py:85
  578.5 9.6 all_gather.21
  588.0 15.8 %fusion.116 = f32[2,64,16,128]{3,1,2,0:T(8,128)S(1)} fusion(bf16[16,128,8192,1]{2,1,0,3:T(8,128)(2,1)} %bitcast.235, bf16[1,2,64,8192]{3,2,1,0:T(8,128)(2,1)S(1)} %copy-done.2, f32[8192]{0:T(1024)S(1)} %bitcast.252, f32[2,64]{1,0:T(2,128)S(1)} %get-tuple-element.23), kind=kOutput, calls=%fused_computation.132 | convolution fusion | flops 4299161600 | bytes 36733440 | tf_op jit(solution)/shard_map/bpd,dc->bpc/dot_general | solution.py:69
  609.8 32.5 %fusion.45 = bf16[2,64,2048]{2,1,0:T(8,128)(2,1)S(1)} fusion(bf16[2,64,8192]{2,1,0:T(8,128)(2,1)} %all-gather.5.cloned.1.call-done, bf16[2048,4096]{1,0:T(8,128)(2,1)} %collective-permute-done.1, bf16[2048,4096]{1,0:T(8,128)(2,1)} %maximum_select_fusion.1, pred[]{:T(512)S(6)} %eq.52), kind=kOutput, calls=%fused_computation.38 | convolution fusion | flops 4446224384 | bytes 36175872 | tf_op jit(solution)/shard_map/bpd,cd->bpc/dot_general | solution.py:81
  645.0 15.5 %fusion.78 = f32[2,2,128,8,64]{2,4,3,1,0:T(8,128)} fusion(f32[2,2,256,64,8]{2,3,4,1,0:T(8,128)} %fusion.97, bf16[2,256,2,128]{3,1,2,0:T(8,128)(2,1)S(1)} %all_gather.20, f32[2,2,8,64,256]{4,3,2,1,0:T(8,128)} %get-tuple-element.29, f32[2,2,8,64]{3,2,1,0:T(8,128)S(1)} %get-tuple-element.28), kind=kOutput, calls=%fused_computation.87 | convolution fusion | flops 137890048 | bytes 5513216 | tf_op jit(solution)/shard_map/bkgpj,bjkd->bpkgd/dot_general | solution.py:112
  668.8 16.3 %fusion.67 = bf16[2,256,2,128]{3,1,2,0:T(8,128)(2,1)} fusion(bf16[2,64,2,8,128]{4,1,3,2,0:T(8,128)(2,1)} %bitcast.256, f32[2,2,256,64,8]{2,3,4,1,0:T(8,128)} %fusion.97, f32[2,2,8,64,256]{4,3,2,1,0:T(8,128)} %get-tuple-element.29, f32[2,2,8,64]{3,2,1,0:T(8,128)S(1)} %get-tuple-element.28), kind=kOutput, calls=%fused_computation.67 | convolution fusion | flops 138021120 | bytes 4988928 | tf_op jit(solution)/shard_map/bkgpj,bpkgd->bjkd/dot_general | solution.py:115
  685.2 24.9 %all-reduce.11.cloned.1.call-done = bf16[2,256,2,128]{3,2,0,1:T(2,128)(2,1)} async-done(((bf16[2,256,2,128]{3,2,0,1:T(2,128)(2,1)}), bf16[2,256,2,128]{3,2,0,1:T(2,128)(2,1)}) %all-reduce.11.cloned.1.call-update) | async-done | bytes 262160
  716.6 20.4 %reduce-scatter.3.cloned.1.call-done = bf16[2,64,2,128]{3,1,2,0:T(8,128)(2,1)} async-done(((bf16[2,256,2,128]{3,1,2,0:T(8,128)(2,1)}), bf16[2,64,2,128]{3,1,2,0:T(8,128)(2,1)}) %reduce-scatter.3.cloned.1.call-update) | async-done | bytes 65552 | tf_op jit(solution)/shard_map/reduce_scatter | solution.py:122
  738.0 5.8 fusion.43
  743.8 19.3 %fusion.27 = bf16[2,64,8192]{2,1,0:T(8,128)(2,1)} fusion(f32[2,64,8192]{2,1,0:T(8,128)} %fusion.39, f32[2,64,8192]{2,1,0:T(8,128)} %fusion.43, bf16[1,8192,2048]{2,1,0:T(8,128)(2,1)} %param.14, f32[2,64,16,64]{3,1,2,0:T(8,128)} %get-tuple-element.12, f32[2,64,16,64]{3,1,2,0:T(8,128)} %get-tuple-element.11, f32[2,64,16,128]{3,1,2,0:T(8,128)S(1)} %bitcast.243, ...), kind=kOutput, calls=%fused_computation.17 | convolution fusion | flops 4299161600 | bytes 46170112 | tf_op jit(solution)/shard_map/bpc,dc->bpd/dot_general | solution.py:138
  763.1 86.2 %all-reduce.7.cloned.1.call-done = bf16[2,64,8192]{2,1,0:T(8,128)(2,1)} async-done(((bf16[2,64,8192]{2,1,0:T(8,128)(2,1)}), bf16[2,64,8192]{2,1,0:T(8,128)(2,1)}) %all-reduce.7.cloned.1.call-update) | async-done | bytes 2097168 | tf_op jit(solution)/shard_map/psum | solution.py:145
  863.1 44.6 %all-gather.7.cloned.1.call-done = bf16[2,64,8192]{2,1,0:T(8,128)(2,1)} async-done(((bf16[2,64,2048]{2,1,0:T(8,128)(2,1)}), bf16[2,64,8192]{2,1,0:T(8,128)(2,1)}) %all-gather.7.cloned.1.call-update) | async-done | bytes 2097168 | tf_op jit(solution)/shard_map/all_gather | solution.py:60
  907.7 32.5 %fusion.48 = bf16[2,64,2048]{2,1,0:T(8,128)(2,1)S(1)} fusion(bf16[2,64,8192]{2,1,0:T(8,128)(2,1)} %all-gather.7.cloned.1.call-done, bf16[2048,4096]{1,0:T(8,128)(2,1)} %collective-permute-done.1, bf16[2048,4096]{1,0:T(8,128)(2,1)} %maximum_select_fusion.1, pred[]{:T(512)S(6)} %eq.52), kind=kOutput, calls=%fused_computation.39 | convolution fusion | flops 4446224384 | bytes 36175872 | tf_op jit(solution)/shard_map/bpd,cd->bpc/dot_general | solution.py:81
  944.8 15.5 %fusion.80 = f32[2,2,128,8,64]{2,4,3,1,0:T(8,128)} fusion(f32[2,2,256,64,8]{2,3,4,1,0:T(8,128)} %fusion.94, bf16[2,256,2,128]{3,1,2,0:T(8,128)(2,1)S(1)} %copy-done.18, f32[2,2,8,64,256]{4,3,2,1,0:T(8,128)} %get-tuple-element.29, f32[2,2,8,64]{3,2,1,0:T(8,128)S(1)} %get-tuple-element.28), kind=kOutput, calls=%fused_computation.89 | convolution fusion | flops 137890048 | bytes 5513216 | tf_op jit(solution)/shard_map/bkgpj,bjkd->bpkgd/dot_general | solution.py:112
  965.2 16.3 %fusion.65 = bf16[2,256,2,128]{3,1,2,0:T(8,128)(2,1)} fusion(bf16[2,64,2,8,128]{4,1,3,2,0:T(8,128)(2,1)} %bitcast.257, f32[2,2,256,64,8]{2,3,4,1,0:T(8,128)} %fusion.94, f32[2,2,8,64,256]{4,3,2,1,0:T(8,128)} %get-tuple-element.29, f32[2,2,8,64]{3,2,1,0:T(8,128)S(1)} %get-tuple-element.28), kind=kOutput, calls=%fused_computation.65 | convolution fusion | flops 138021120 | bytes 4988928 | tf_op jit(solution)/shard_map/bkgpj,bpkgd->bjkd/dot_general | solution.py:115
  981.9 23.8 %all-reduce.13.cloned.1.call-done = bf16[2,256,2,128]{3,2,0,1:T(2,128)(2,1)} async-done(((bf16[2,256,2,128]{3,2,0,1:T(2,128)(2,1)}), bf16[2,256,2,128]{3,2,0,1:T(2,128)(2,1)}) %all-reduce.13.cloned.1.call-update) | async-done | bytes 262160
  1012.2 20.5 %reduce-scatter.5.cloned.1.call-done = bf16[2,64,2,128]{3,1,2,0:T(8,128)(2,1)} async-done(((bf16[2,256,2,128]{3,1,2,0:T(8,128)(2,1)}), bf16[2,64,2,128]{3,1,2,0:T(8,128)(2,1)}) %reduce-scatter.5.cloned.1.call-update) | async-done | bytes 65552 | tf_op jit(solution)/shard_map/reduce_scatter | solution.py:122
  1039.5 19.2 %fusion.24 = bf16[2,64,8192]{2,1,0:T(8,128)(2,1)} fusion(f32[2,64,8192]{2,1,0:T(8,128)} %fusion.37, f32[2,64,8192]{2,1,0:T(8,128)} %fusion.41, bf16[1,8192,2048]{2,1,0:T(8,128)(2,1)} %param.14, f32[2,64,16,64]{3,1,2,0:T(8,128)} %get-tuple-element.10, f32[2,64,16,64]{3,1,2,0:T(8,128)} %get-tuple-element.9, f32[2,64,16,128]{3,1,2,0:T(8,128)S(1)} %bitcast.241, ...), kind=kOutput, calls=%fused_computation.16 | convolution fusion | flops 4299161600 | bytes 46170112 | tf_op jit(solution)/shard_map/bpc,dc->bpd/dot_general | solution.py:138
  1058.7 86.3 %all-reduce.9.cloned.1.call-done = bf16[2,64,8192]{2,1,0:T(8,128)(2,1)} async-done(((bf16[2,64,8192]{2,1,0:T(8,128)(2,1)}), bf16[2,64,8192]{2,1,0:T(8,128)(2,1)}) %all-reduce.9.cloned.1.call-update) | async-done | bytes 2097168 | tf_op jit(solution)/shard_map/psum | solution.py:145
  (119 shorter events, 83.1 us)
Async XLA Ops:
  6.5 206.1 %copy-start = (bf16[2,32,2048]{2,1,0:T(8,128)(2,1)S(1)}, bf16[2,32,2048]{2,1,0:T(8,128)(2,1)}, u32[]{:S(2)}) copy-start(bf16[2,32,2048]{2,1,0:T(8,128)(2,1)} %param.10) | copy-start | bytes 786436
  6.5 262.8 %all-gather.9.cloned.1.call-start = ((), (), s32[]{:S(2)}) async-start(), calls=%async_computation.8 | async-start | bytes 2621440 | tf_op jit(solution)/shard_map/all_gather | solution.py:59
  6.5 183.7 %collective-permute-start = (bf16[2048,2048]{1,0:T(8,128)(2,1)}, bf16[2048,2048]{1,0:T(8,128)(2,1)}, u32[]{:S(2)}, u32[]{:S(2)}) collective-permute-start(bf16[2048,2048]{1,0:T(8,128)(2,1)} %bitcast.238), channel_id=1, source_target_pairs={{0,8},{8,0},{16,24},{24,16},{1,9},{9,1},{17,25},{25,17},{2,10},{10... | collective-permute-start | bytes 25165832 | tf_op jit(solution)/shard_map/ppermute | solution.py:16
  9.5 203.1 %copy-start.19 = (s32[2,32]{1,0:T(2,128)S(1)}, s32[2,32]{1,0:T(2,128)}, u32[]{:S(2)}) copy-start(s32[2,32]{1,0:T(2,128)} %param.11) | copy-start | bytes 772
  210.7 399.0 %collective-permute-start.1 = (bf16[2048,4096]{1,0:T(8,128)(2,1)}, bf16[2048,4096]{1,0:T(8,128)(2,1)}, u32[]{:S(2)}, u32[]{:S(2)}) collective-permute-start(bf16[2048,4096]{1,0:T(8,128)(2,1)} %maximum_select_fusion.1), channel_id=1, source_target_pairs={{0,16},{8,24},{16,0},{24,8},{1,17},{9,25},{17,1},{25,9},{2,18},{10... | collective-permute-start | bytes 50331656 | tf_op jit(solution)/shard_map/ppermute | solution.py:16
  212.5 397.2 %all-gather.5.cloned.1.call-start = ((), (), s32[]{:S(2)}) async-start(), calls=%async_computation.2 | async-start | bytes 2621440 | tf_op jit(solution)/shard_map/all_gather | solution.py:60
  213.9 496.1 %all-reduce.11.cloned.1.call-start = ((), (), s32[]{:S(2)}) async-start(), calls=%async_computation.9 | async-start | bytes 524288
  261.0 6.5 copy-start.21
  261.0 8.0 copy-start.20
  261.0 10.4 copy-start.14
  271.5 305.4 %copy-start.2 = (bf16[1,2,64,8192]{3,2,1,0:T(8,128)(2,1)S(1)}, bf16[1,2,64,8192]{3,2,1,0:T(8,128)(2,1)}, u32[]{:S(2)}) copy-start(bf16[1,2,64,8192]{3,2,1,0:T(8,128)(2,1)} %all-gather.9.cloned.1.call-done) | copy-start | bytes 6291460
  271.5 305.4 %copy-start.9 = (bf16[256,8192]{1,0:T(8,128)(2,1)S(1)}, bf16[256,8192]{1,0:T(8,128)(2,1)}, u32[]{:S(2)}) copy-start(bf16[256,8192]{1,0:T(8,128)(2,1)} %copy.64) | copy-start | bytes 12582916
  576.9 68.1 %copy-start.17 = (bf16[2,256,2,128]{3,1,2,0:T(8,128)(2,1)}, bf16[2,256,2,128]{3,1,2,0:T(8,128)(2,1)S(1)}, u32[]{:S(2)}) copy-start(bf16[2,256,2,128]{3,1,2,0:T(8,128)(2,1)S(1)} %all_gather.20) | copy-start | bytes 786436
  588.0 54.4 %copy-start.11 = (bf16[2,256,2,128]{3,1,2,0:T(8,128)(2,1)}, bf16[2,256,2,128]{3,1,2,0:T(8,128)(2,1)S(1)}, u32[]{:S(2)}) copy-start(bf16[2,256,2,128]{3,1,2,0:T(8,128)(2,1)S(1)} %all_gather.21) | copy-start | bytes 786436
  604.6 37.6 %copy-start.15 = (bf16[2,64,16,128]{3,1,2,0:T(8,128)(2,1)}, bf16[2,64,16,128]{3,1,2,0:T(8,128)(2,1)S(1)}, u32[]{:S(2)}) copy-start(bf16[2,64,16,128]{3,1,2,0:T(8,128)(2,1)S(1)} %fusion.75) | copy-start | bytes 1572868
  666.5 70.5 %reduce-scatter.3.cloned.1.call-start = ((), (), s32[]{:S(2)}) async-start(), calls=%async_computation.3 | async-start | bytes 327680 | tf_op jit(solution)/shard_map/reduce_scatter | solution.py:122
  685.1 164.2 %all-reduce.7.cloned.1.call-start = ((), (), s32[]{:S(2)}) async-start(), calls=%async_computation.4 | async-start | bytes 4194304 | tf_op jit(solution)/shard_map/psum | solution.py:145
  763.0 144.6 %all-gather.7.cloned.1.call-start = ((), (), s32[]{:S(2)}) async-start(), calls=%async_computation.5 | async-start | bytes 2621440 | tf_op jit(solution)/shard_map/all_gather | solution.py:60
  858.2 3.8 collective-permute-start.2
  862.8 77.5 %copy-start.12 = (bf16[2,256,2,128]{3,1,2,0:T(8,128)(2,1)S(1)}, bf16[2,256,2,128]{3,1,2,0:T(8,128)(2,1)}, u32[]{:S(2)}) copy-start(bf16[2,256,2,128]{3,1,2,0:T(8,128)(2,1)} %copy-done.11) | copy-start | bytes 786436
  862.9 142.8 %all-reduce.13.cloned.1.call-start = ((), (), s32[]{:S(2)}) async-start(), calls=%async_computation.10 | async-start | bytes 524288
  963.5 69.2 %reduce-scatter.5.cloned.1.call-start = ((), (), s32[]{:S(2)}) async-start(), calls=%async_computation.6 | async-start | bytes 327680 | tf_op jit(solution)/shard_map/reduce_scatter | solution.py:122
  981.6 163.4 %all-reduce.9.cloned.1.call-start = ((), (), s32[]{:S(2)}) async-start(), calls=%async_computation.7 | async-start | bytes 4194304 | tf_op jit(solution)/shard_map/psum | solution.py:145
  1058.7 89.4 %copy-start.10 = (f32[2,64,2048]{2,1,0:T(8,128)S(1)}, f32[2,64,2048]{2,1,0:T(8,128)}, u32[]{:S(2)}) copy-start(f32[2,64,2048]{2,1,0:T(8,128)} %get-tuple-element.6) | copy-start | bytes 3145732
  (10 other events, 35.1 us)
Sparse Core Ops, SparseCore 0:
  212.7 45.9 all-gather.8
  260.2 44.4 all-gather.4
  666.6 43.3 all-reduce.10
  712.6 24.3 reduce-scatter.2
  763.2 86.1 all-reduce.6
  863.0 44.6 all-gather.6
  963.6 41.9 all-reduce.12
  1008.4 24.3 reduce-scatter.4
  1058.8 86.1 all-reduce.8
